TPU v7x, 256 devices: a whole 4x4x8 slice. The times are simulated.
256 devices in a mesh: dp: 8 (over y, x_hi), ctx: 32 (over x_lo, z, core).
Axes of the slice: x: 4 (x_hi: 2, x_lo: 2; x = x_hi * 2 + x_lo), y: 4, z: 8, core: 2. Of those that a mesh axis runs over, the one named last changes fastest.
Arguments:
- inputs: bfloat16 [8, 32, 128, 4096], P('dp', 'ctx'), may hold values from -6 to 6
- queries: bfloat16 [8, 32, 128, 1024], P('dp', 'ctx'), may hold values from -6 to 6
- keys_values: bfloat16 [8, 32, 128, 256], P('dp', 'ctx'), may hold values from -6 to 6
- out_grad: bfloat16 [8, 32, 128, 1024], P('dp', 'ctx'), may hold values from -6 to 6
- lengths: int32 [8, 10], P('dp'), may hold values from 1 to 1024, 4096 in all within a row
Outputs:
- grad_q: bfloat16 [8, 32, 128, 1024], P('dp', 'ctx')
- grad_kv: bfloat16 [8, 32, 128, 256], P('dp', 'ctx')
- grad_kv_weight: float32 [4096, 256], P('ctx')
All inputs are finite; a program needn't handle non-finite values.
Results may differ from a plain program's by a relative error of at most 0.0052.
Values may be sent and summed in bfloat16 or wider, within the bound.
A program may use at most 64 MiB of HBM per device.

v0:
```python
import jax
import jax.numpy as jnp
from jax import lax
from jax.sharding import PartitionSpec as P

HD = 128
RESPONSES = 4
neg_fill = -1e30


def from_behind(x, axis, by):
    length = lax.axis_size(axis)
    return lax.ppermute(x, axis, [(i, (i + by) % length) for i in range(length)])


def piece_of(positions, piece_ends):
    return jnp.sum((positions[:, None] >= piece_ends[None, :]).astype(jnp.int32), axis=1)


def allowed_pairs(query_pos, key_pos, piece_ends):
    per_group = RESPONSES + 1
    query_piece = piece_of(query_pos, piece_ends)
    key_piece = piece_of(key_pos, piece_ends)
    same_group = (query_piece // per_group)[:, None] == (key_piece // per_group)[None, :]
    visible = (key_piece % per_group == 0)[None, :] | (query_piece[:, None] == key_piece[None, :])
    return (key_pos[None, :] <= query_pos[:, None]) & same_group & visible


def contract_rows(left_side, right_side):
    return lax.dot_general(
        left_side, right_side, (((0,), (0,)), ((), ())), preferred_element_type=jnp.float32
    )


def on_device(inputs, queries, keys_values, out_grad, lengths):
    stripe_count = lax.axis_size("ctx")
    my_stripe = lax.axis_index("ctx")
    local_count = queries.shape[2]
    q_width = queries.shape[3]
    head_count = q_width // HD
    row_total = local_count * head_count
    score_scale = HD ** (-0.5)
    x_local = inputs[0, 0]
    q_rows = queries[0, 0].reshape(row_total, HD)
    grad_rows = out_grad[0, 0].reshape(row_total, HD)
    kv_local = keys_values[0, 0]
    piece_ends = jnp.cumsum(lengths[0], dtype=jnp.int32)
    query_pos = jnp.arange(local_count, dtype=jnp.int32) * stripe_count + my_stripe

    def row_mask(key_pos):
        key_count = key_pos.shape[0]
        allowed = allowed_pairs(query_pos, key_pos, piece_ends)
        return jnp.broadcast_to(allowed[:, None, :], (local_count, head_count, key_count)).reshape(
            row_total, key_count
        )

    def gathered_pos(first_row, row_count):
        key_rows = first_row + jnp.arange(row_count, dtype=jnp.int32)
        return key_rows % local_count * stripe_count + key_rows // local_count

    def forward_block(carried, kv_block, key_pos):
        running_max, running_sum, weighted = carried
        allowed = row_mask(key_pos)
        scores = (
            jnp.dot(q_rows, kv_block[:, :HD].T, preferred_element_type=jnp.float32) * score_scale
        )
        prob_grad = jnp.dot(grad_rows, kv_block[:, HD:].T, preferred_element_type=jnp.float32)
        new_max = jnp.maximum(running_max, jnp.max(jnp.where(allowed, scores, neg_fill), axis=1))
        factor = jnp.exp(running_max - new_max)
        expo_terms = jnp.where(allowed, jnp.exp(scores - new_max[:, None]), 0.0)
        new_sum = running_sum * factor + jnp.sum(expo_terms, axis=1)
        new_weighted = weighted * factor + jnp.sum(expo_terms * prob_grad, axis=1)
        return (new_max, new_sum, new_weighted)

    init_state = (
        jnp.full((row_total,), neg_fill, jnp.float32),
        jnp.zeros((row_total,), jnp.float32),
        jnp.zeros((row_total,), jnp.float32),
    )
    carried = init_state
    kv_piece = lax.all_gather(kv_local, "ctx", axis=0, tiled=True)
    row_count = kv_piece.shape[0]
    sub_blocks = kv_piece.reshape(row_count // 512, 512, kv_piece.shape[1])

    def inner_step(state_now, sub_item):
        sub_block, sub_index = sub_item
        return (forward_block(state_now, sub_block, gathered_pos(sub_index * 512, 512)), None)

    carried, unused = lax.scan(
        inner_step, carried, (sub_blocks, jnp.arange(row_count // 512, dtype=jnp.int32))
    )
    running_max, running_sum, weighted = carried
    log_total = running_max + jnp.log(running_sum)
    row_delta = weighted / running_sum

    def backward_block(grad_q, kv_block, key_pos):
        allowed = row_mask(key_pos)
        scores = (
            jnp.dot(q_rows, kv_block[:, :HD].T, preferred_element_type=jnp.float32) * score_scale
        )
        soft_probs = jnp.where(allowed, jnp.exp(scores - log_total[:, None]), 0.0)
        prob_grad = jnp.dot(grad_rows, kv_block[:, HD:].T, preferred_element_type=jnp.float32)
        score_grad = soft_probs * (prob_grad - row_delta[:, None])
        low_probs = soft_probs.astype(jnp.bfloat16)
        low_score = score_grad.astype(jnp.bfloat16)
        grad_q = (
            grad_q
            + jnp.dot(low_score, kv_block[:, :HD], preferred_element_type=jnp.float32) * score_scale
        )
        key_term = contract_rows(low_score, q_rows) * score_scale
        value_term = contract_rows(low_probs, grad_rows)
        return (grad_q, jnp.concatenate([key_term, value_term], axis=1))

    zero_grad = jnp.zeros((row_total, HD), jnp.float32)

    def cycle_step(cycle_index, state_now):
        grad_q, kv_block, key_grads = state_now
        source = (my_stripe - cycle_index) % stripe_count
        key_pos = jnp.arange(local_count, dtype=jnp.int32) * stripe_count + source
        grad_q, key_term = backward_block(grad_q, kv_block, key_pos)
        kv_block = from_behind(kv_block, "ctx", 1)
        key_grads = from_behind(key_grads + key_term, "ctx", 1)
        return (grad_q, kv_block, key_grads)

    def cycle_pair(pair_index, state_now):
        return cycle_step(2 * pair_index + 1, cycle_step(2 * pair_index, state_now))

    start_state = (zero_grad, kv_local, jnp.zeros((local_count, 2 * HD), jnp.float32))
    grad_q, spent_kv, key_grads = lax.fori_loop(0, stripe_count // 2, cycle_pair, start_state)
    kv_grad_low = key_grads.astype(jnp.bfloat16)
    grad_q_out = grad_q.astype(jnp.bfloat16).reshape(1, 1, local_count, q_width)
    dp_count = lax.axis_size("dp")
    weight_shard = lax.psum_scatter(
        contract_rows(x_local, kv_grad_low), "ctx", scatter_dimension=0, tiled=True
    )
    weight_total = lax.psum(weight_shard, "dp")
    return (grad_q_out, kv_grad_low.reshape(1, 1, local_count, 2 * HD), weight_total / dp_count)


def solution(mesh):
    return jax.shard_map(
        on_device,
        mesh=mesh,
        in_specs=(
            P("dp", "ctx", None, None),
            P("dp", "ctx", None, None),
            P("dp", "ctx", None, None),
            P("dp", "ctx", None, None),
            P("dp", None),
        ),
        out_specs=(P("dp", "ctx", None, None), P("dp", "ctx", None, None), P("ctx", None)),
        check_vma=False,
    )
```

profile of v0, /device:TPU:32, one launch (start us, length us, event | category | flops | bytes accessed | tf_op | source)
XLA Modules:
  0.0 600.0 jit_solution(14512297040010059716)
XLA Ops:
  12.6 64.4 %all-gather.3.cloned.1.call-done = bf16[1,1,4096,256]{3,2,1,0:T(8,128)(2,1)} async-done(((bf16[1,1,128,256]{3,2,1,0:T(8,128)(2,1)}), bf16[1,1,4096,256]{3,2,1,0:T(8,128)(2,1)}) %all-gather.3.cloned.1.call-update) | async-done | bytes 2097168 | tf_op jit(solution)/shard_map/all_gather | solution.py:81
  77.0 55.5 %while.41 = (s32[]{:T(128)}, f32[1024]{0:T(1024)S(1)}, f32[1024]{0:T(1024)S(1)}, f32[1024]{0:T(1024)S(1)}, s32[8]{0:T(128)S(1)}, /*index=5*/s32[10]{0:T(128)S(1)...) while((s32[]{:T(128)}, f32[1024]{0:T(1024)S(1)}, ...), condition=%wide.region_7.8_spmd.clone, body=%wide.region_1.7_spmd.clone.sunk | while | flops 275166080 | bytes 18316680 | solution.py:89
  132.5 242.1 %while.42 = (s32[]{:T(128)}, f32[1024,128]{1,0:T(8,128)}, bf16[128,256]{1,0:T(8,128)(2,1)S(1)}, f32[128,256]{0,1:T(8,128)S(1)}, s32[]{:T(128)}, /*index=5*/s32[1...) while((s32[]{:T(128)}, f32[1024,128]{1,0:T(8,128)}, ...), condition=%wide.region_12.13_spmd.clone.clone.clone, body=%wide.region_8.12_spmd.clone.clone.clone.sunk | while | flops 338411936 | bytes 14973101 | solution.py:129
  166.1 3.0 collective-permute-done.1
  174.3 3.0 collective-permute-done
  181.7 3.0 collective-permute-done.1
  189.9 3.0 collective-permute-done
  197.3 3.0 collective-permute-done.1
  205.6 3.0 collective-permute-done
  212.9 3.0 collective-permute-done.1
  221.2 3.0 collective-permute-done
  228.5 3.0 collective-permute-done.1
  236.8 3.0 collective-permute-done
  244.2 3.0 collective-permute-done.1
  252.4 3.0 collective-permute-done
  259.8 3.0 collective-permute-done.1
  268.0 3.0 collective-permute-done
  275.4 3.0 collective-permute-done.1
  283.7 3.0 collective-permute-done
  291.0 3.0 collective-permute-done.1
  299.3 3.0 collective-permute-done
  306.6 3.0 collective-permute-done.1
  314.9 3.0 collective-permute-done
  322.3 3.0 collective-permute-done.1
  330.5 3.0 collective-permute-done
  337.9 3.0 collective-permute-done.1
  346.1 3.0 collective-permute-done
  353.5 3.0 collective-permute-done.1
  361.8 3.0 collective-permute-done
  369.1 3.0 collective-permute-done.1
  377.5 123.0 %reduce-scatter.2.cloned.1.call-done = f32[128,256]{0,1:T(8,128)} async-done(((f32[4096,256]{0,1:T(8,128)}), f32[128,256]{0,1:T(8,128)}) %reduce-scatter.2.cloned.1.call-update) | async-done | bytes 131088 | tf_op jit(solution)/shard_map/reduce_scatter | solution.py:133
  501.4 90.5 %all-reduce.2.cloned.1.call-done = f32[128,256]{0,1:T(8,128)} async-done(((f32[128,256]{0,1:T(8,128)}), f32[128,256]{0,1:T(8,128)}) %all-reduce.2.cloned.1.call-update) | async-done | bytes 131088 | tf_op jit(solution)/shard_map/psum | solution.py:136
  (740 shorter events, 218.4 us)
Async XLA Ops:
  7.2 69.8 %all-gather.3.cloned.1.call-start = ((), (), s32[]{:S(2)}) async-start(), calls=%async_computation.3 | async-start | bytes 2162688 | tf_op jit(solution)/shard_map/all_gather | solution.py:81
  8.8 491.7 %reduce-scatter.2.cloned.1.call-start = ((), (), s32[]{:S(2)}) async-start(), calls=%async_computation.1 | async-start | bytes 4325376 | tf_op jit(solution)/shard_map/reduce_scatter | solution.py:133
  158.4 6.6 %collective-permute-start.2 = (f32[128,256]{0,1:T(8,128)S(1)}, f32[128,256]{0,1:T(8,128)S(1)}, u32[]{:S(2)}, u32[]{:S(2)}) collective-permute-start(f32[128,256]{0,1:T(8,128)S(1)} %maximum_add_fusion.4), channel_id=1, source_target_pairs={{0,1},{1,2},{2,3},{3,4},{4,5},{5,6},{6,7},{7,8},{8,9},{9,10},{10,1... | collective-permute-start | bytes 393224 | tf_op jit(solution)/shard_map/while/body/eval_jaxpr/ppermute | solution.py:13
  162.6 6.5 %collective-permute-start.1 = (bf16[128,256]{1,0:T(8,128)(2,1)S(1)}, bf16[128,256]{1,0:T(8,128)(2,1)S(1)}, u32[]{:S(2)}, u32[]{:S(2)}) collective-permute-start(bf16[128,256]{1,0:T(8,128)(2,1)S(1)} %collective-permute-done), channel_id=1, source_target_pairs={{0,1},{1,2},{2,3},{3,4},{4,5},{5,6},{6,7},{7,8},{8,9},{9,10},{10,1... | collective-permute-start | bytes 196616 | tf_op jit(solution)/shard_map/while/body/eval_jaxpr/ppermute | solution.py:13
  165.0 6.6 %collective-permute-start.3 = (f32[128,256]{0,1:T(8,128)S(1)}, f32[128,256]{0,1:T(8,128)S(1)}, u32[]{:S(2)}, u32[]{:S(2)}) collective-permute-start(f32[128,256]{0,1:T(8,128)S(1)} %maximum_add_fusion.5), channel_id=1, source_target_pairs={{0,1},{1,2},{2,3},{3,4},{4,5},{5,6},{6,7},{7,8},{8,9},{9,10},{10,1... | collective-permute-start | bytes 393224 | tf_op jit(solution)/shard_map/while/body/eval_jaxpr/ppermute | solution.py:13
  174.0 6.6 %collective-permute-start.2 = (f32[128,256]{0,1:T(8,128)S(1)}, f32[128,256]{0,1:T(8,128)S(1)}, u32[]{:S(2)}, u32[]{:S(2)}) collective-permute-start(f32[128,256]{0,1:T(8,128)S(1)} %maximum_add_fusion.4), channel_id=1, source_target_pairs={{0,1},{1,2},{2,3},{3,4},{4,5},{5,6},{6,7},{7,8},{8,9},{9,10},{10,1... | collective-permute-start | bytes 393224 | tf_op jit(solution)/shard_map/while/body/eval_jaxpr/ppermute | solution.py:13
  180.6 6.6 %collective-permute-start.3 = (f32[128,256]{0,1:T(8,128)S(1)}, f32[128,256]{0,1:T(8,128)S(1)}, u32[]{:S(2)}, u32[]{:S(2)}) collective-permute-start(f32[128,256]{0,1:T(8,128)S(1)} %maximum_add_fusion.5), channel_id=1, source_target_pairs={{0,1},{1,2},{2,3},{3,4},{4,5},{5,6},{6,7},{7,8},{8,9},{9,10},{10,1... | collective-permute-start | bytes 393224 | tf_op jit(solution)/shard_map/while/body/eval_jaxpr/ppermute | solution.py:13
  189.6 6.6 %collective-permute-start.2 = (f32[128,256]{0,1:T(8,128)S(1)}, f32[128,256]{0,1:T(8,128)S(1)}, u32[]{:S(2)}, u32[]{:S(2)}) collective-permute-start(f32[128,256]{0,1:T(8,128)S(1)} %maximum_add_fusion.4), channel_id=1, source_target_pairs={{0,1},{1,2},{2,3},{3,4},{4,5},{5,6},{6,7},{7,8},{8,9},{9,10},{10,1... | collective-permute-start | bytes 393224 | tf_op jit(solution)/shard_map/while/body/eval_jaxpr/ppermute | solution.py:13
  196.2 6.6 %collective-permute-start.3 = (f32[128,256]{0,1:T(8,128)S(1)}, f32[128,256]{0,1:T(8,128)S(1)}, u32[]{:S(2)}, u32[]{:S(2)}) collective-permute-start(f32[128,256]{0,1:T(8,128)S(1)} %maximum_add_fusion.5), channel_id=1, source_target_pairs={{0,1},{1,2},{2,3},{3,4},{4,5},{5,6},{6,7},{7,8},{8,9},{9,10},{10,1... | collective-permute-start | bytes 393224 | tf_op jit(solution)/shard_map/while/body/eval_jaxpr/ppermute | solution.py:13
  205.2 6.6 %collective-permute-start.2 = (f32[128,256]{0,1:T(8,128)S(1)}, f32[128,256]{0,1:T(8,128)S(1)}, u32[]{:S(2)}, u32[]{:S(2)}) collective-permute-start(f32[128,256]{0,1:T(8,128)S(1)} %maximum_add_fusion.4), channel_id=1, source_target_pairs={{0,1},{1,2},{2,3},{3,4},{4,5},{5,6},{6,7},{7,8},{8,9},{9,10},{10,1... | collective-permute-start | bytes 393224 | tf_op jit(solution)/shard_map/while/body/eval_jaxpr/ppermute | solution.py:13
  211.8 6.6 %collective-permute-start.3 = (f32[128,256]{0,1:T(8,128)S(1)}, f32[128,256]{0,1:T(8,128)S(1)}, u32[]{:S(2)}, u32[]{:S(2)}) collective-permute-start(f32[128,256]{0,1:T(8,128)S(1)} %maximum_add_fusion.5), channel_id=1, source_target_pairs={{0,1},{1,2},{2,3},{3,4},{4,5},{5,6},{6,7},{7,8},{8,9},{9,10},{10,1... | collective-permute-start | bytes 393224 | tf_op jit(solution)/shard_map/while/body/eval_jaxpr/ppermute | solution.py:13
  220.9 6.6 %collective-permute-start.2 = (f32[128,256]{0,1:T(8,128)S(1)}, f32[128,256]{0,1:T(8,128)S(1)}, u32[]{:S(2)}, u32[]{:S(2)}) collective-permute-start(f32[128,256]{0,1:T(8,128)S(1)} %maximum_add_fusion.4), channel_id=1, source_target_pairs={{0,1},{1,2},{2,3},{3,4},{4,5},{5,6},{6,7},{7,8},{8,9},{9,10},{10,1... | collective-permute-start | bytes 393224 | tf_op jit(solution)/shard_map/while/body/eval_jaxpr/ppermute | solution.py:13
  227.4 6.6 %collective-permute-start.3 = (f32[128,256]{0,1:T(8,128)S(1)}, f32[128,256]{0,1:T(8,128)S(1)}, u32[]{:S(2)}, u32[]{:S(2)}) collective-permute-start(f32[128,256]{0,1:T(8,128)S(1)} %maximum_add_fusion.5), channel_id=1, source_target_pairs={{0,1},{1,2},{2,3},{3,4},{4,5},{5,6},{6,7},{7,8},{8,9},{9,10},{10,1... | collective-permute-start | bytes 393224 | tf_op jit(solution)/shard_map/while/body/eval_jaxpr/ppermute | solution.py:13
  236.5 6.6 %collective-permute-start.2 = (f32[128,256]{0,1:T(8,128)S(1)}, f32[128,256]{0,1:T(8,128)S(1)}, u32[]{:S(2)}, u32[]{:S(2)}) collective-permute-start(f32[128,256]{0,1:T(8,128)S(1)} %maximum_add_fusion.4), channel_id=1, source_target_pairs={{0,1},{1,2},{2,3},{3,4},{4,5},{5,6},{6,7},{7,8},{8,9},{9,10},{10,1... | collective-permute-start | bytes 393224 | tf_op jit(solution)/shard_map/while/body/eval_jaxpr/ppermute | solution.py:13
  243.1 6.6 %collective-permute-start.3 = (f32[128,256]{0,1:T(8,128)S(1)}, f32[128,256]{0,1:T(8,128)S(1)}, u32[]{:S(2)}, u32[]{:S(2)}) collective-permute-start(f32[128,256]{0,1:T(8,128)S(1)} %maximum_add_fusion.5), channel_id=1, source_target_pairs={{0,1},{1,2},{2,3},{3,4},{4,5},{5,6},{6,7},{7,8},{8,9},{9,10},{10,1... | collective-permute-start | bytes 393224 | tf_op jit(solution)/shard_map/while/body/eval_jaxpr/ppermute | solution.py:13
  252.1 6.6 %collective-permute-start.2 = (f32[128,256]{0,1:T(8,128)S(1)}, f32[128,256]{0,1:T(8,128)S(1)}, u32[]{:S(2)}, u32[]{:S(2)}) collective-permute-start(f32[128,256]{0,1:T(8,128)S(1)} %maximum_add_fusion.4), channel_id=1, source_target_pairs={{0,1},{1,2},{2,3},{3,4},{4,5},{5,6},{6,7},{7,8},{8,9},{9,10},{10,1... | collective-permute-start | bytes 393224 | tf_op jit(solution)/shard_map/while/body/eval_jaxpr/ppermute | solution.py:13
  258.7 6.6 %collective-permute-start.3 = (f32[128,256]{0,1:T(8,128)S(1)}, f32[128,256]{0,1:T(8,128)S(1)}, u32[]{:S(2)}, u32[]{:S(2)}) collective-permute-start(f32[128,256]{0,1:T(8,128)S(1)} %maximum_add_fusion.5), channel_id=1, source_target_pairs={{0,1},{1,2},{2,3},{3,4},{4,5},{5,6},{6,7},{7,8},{8,9},{9,10},{10,1... | collective-permute-start | bytes 393224 | tf_op jit(solution)/shard_map/while/body/eval_jaxpr/ppermute | solution.py:13
  267.7 6.6 %collective-permute-start.2 = (f32[128,256]{0,1:T(8,128)S(1)}, f32[128,256]{0,1:T(8,128)S(1)}, u32[]{:S(2)}, u32[]{:S(2)}) collective-permute-start(f32[128,256]{0,1:T(8,128)S(1)} %maximum_add_fusion.4), channel_id=1, source_target_pairs={{0,1},{1,2},{2,3},{3,4},{4,5},{5,6},{6,7},{7,8},{8,9},{9,10},{10,1... | collective-permute-start | bytes 393224 | tf_op jit(solution)/shard_map/while/body/eval_jaxpr/ppermute | solution.py:13
  274.3 6.6 %collective-permute-start.3 = (f32[128,256]{0,1:T(8,128)S(1)}, f32[128,256]{0,1:T(8,128)S(1)}, u32[]{:S(2)}, u32[]{:S(2)}) collective-permute-start(f32[128,256]{0,1:T(8,128)S(1)} %maximum_add_fusion.5), channel_id=1, source_target_pairs={{0,1},{1,2},{2,3},{3,4},{4,5},{5,6},{6,7},{7,8},{8,9},{9,10},{10,1... | collective-permute-start | bytes 393224 | tf_op jit(solution)/shard_map/while/body/eval_jaxpr/ppermute | solution.py:13
  283.3 6.6 %collective-permute-start.2 = (f32[128,256]{0,1:T(8,128)S(1)}, f32[128,256]{0,1:T(8,128)S(1)}, u32[]{:S(2)}, u32[]{:S(2)}) collective-permute-start(f32[128,256]{0,1:T(8,128)S(1)} %maximum_add_fusion.4), channel_id=1, source_target_pairs={{0,1},{1,2},{2,3},{3,4},{4,5},{5,6},{6,7},{7,8},{8,9},{9,10},{10,1... | collective-permute-start | bytes 393224 | tf_op jit(solution)/shard_map/while/body/eval_jaxpr/ppermute | solution.py:13
  289.9 6.6 %collective-permute-start.3 = (f32[128,256]{0,1:T(8,128)S(1)}, f32[128,256]{0,1:T(8,128)S(1)}, u32[]{:S(2)}, u32[]{:S(2)}) collective-permute-start(f32[128,256]{0,1:T(8,128)S(1)} %maximum_add_fusion.5), channel_id=1, source_target_pairs={{0,1},{1,2},{2,3},{3,4},{4,5},{5,6},{6,7},{7,8},{8,9},{9,10},{10,1... | collective-permute-start | bytes 393224 | tf_op jit(solution)/shard_map/while/body/eval_jaxpr/ppermute | solution.py:13
  299.0 6.6 %collective-permute-start.2 = (f32[128,256]{0,1:T(8,128)S(1)}, f32[128,256]{0,1:T(8,128)S(1)}, u32[]{:S(2)}, u32[]{:S(2)}) collective-permute-start(f32[128,256]{0,1:T(8,128)S(1)} %maximum_add_fusion.4), channel_id=1, source_target_pairs={{0,1},{1,2},{2,3},{3,4},{4,5},{5,6},{6,7},{7,8},{8,9},{9,10},{10,1... | collective-permute-start | bytes 393224 | tf_op jit(solution)/shard_map/while/body/eval_jaxpr/ppermute | solution.py:13
  305.6 6.6 %collective-permute-start.3 = (f32[128,256]{0,1:T(8,128)S(1)}, f32[128,256]{0,1:T(8,128)S(1)}, u32[]{:S(2)}, u32[]{:S(2)}) collective-permute-start(f32[128,256]{0,1:T(8,128)S(1)} %maximum_add_fusion.5), channel_id=1, source_target_pairs={{0,1},{1,2},{2,3},{3,4},{4,5},{5,6},{6,7},{7,8},{8,9},{9,10},{10,1... | collective-permute-start | bytes 393224 | tf_op jit(solution)/shard_map/while/body/eval_jaxpr/ppermute | solution.py:13
  314.6 6.6 %collective-permute-start.2 = (f32[128,256]{0,1:T(8,128)S(1)}, f32[128,256]{0,1:T(8,128)S(1)}, u32[]{:S(2)}, u32[]{:S(2)}) collective-permute-start(f32[128,256]{0,1:T(8,128)S(1)} %maximum_add_fusion.4), channel_id=1, source_target_pairs={{0,1},{1,2},{2,3},{3,4},{4,5},{5,6},{6,7},{7,8},{8,9},{9,10},{10,1... | collective-permute-start | bytes 393224 | tf_op jit(solution)/shard_map/while/body/eval_jaxpr/ppermute | solution.py:13
  321.2 6.6 %collective-permute-start.3 = (f32[128,256]{0,1:T(8,128)S(1)}, f32[128,256]{0,1:T(8,128)S(1)}, u32[]{:S(2)}, u32[]{:S(2)}) collective-permute-start(f32[128,256]{0,1:T(8,128)S(1)} %maximum_add_fusion.5), channel_id=1, source_target_pairs={{0,1},{1,2},{2,3},{3,4},{4,5},{5,6},{6,7},{7,8},{8,9},{9,10},{10,1... | collective-permute-start | bytes 393224 | tf_op jit(solution)/shard_map/while/body/eval_jaxpr/ppermute | solution.py:13
  330.2 6.6 %collective-permute-start.2 = (f32[128,256]{0,1:T(8,128)S(1)}, f32[128,256]{0,1:T(8,128)S(1)}, u32[]{:S(2)}, u32[]{:S(2)}) collective-permute-start(f32[128,256]{0,1:T(8,128)S(1)} %maximum_add_fusion.4), channel_id=1, source_target_pairs={{0,1},{1,2},{2,3},{3,4},{4,5},{5,6},{6,7},{7,8},{8,9},{9,10},{10,1... | collective-permute-start | bytes 393224 | tf_op jit(solution)/shard_map/while/body/eval_jaxpr/ppermute | solution.py:13
  336.8 6.6 %collective-permute-start.3 = (f32[128,256]{0,1:T(8,128)S(1)}, f32[128,256]{0,1:T(8,128)S(1)}, u32[]{:S(2)}, u32[]{:S(2)}) collective-permute-start(f32[128,256]{0,1:T(8,128)S(1)} %maximum_add_fusion.5), channel_id=1, source_target_pairs={{0,1},{1,2},{2,3},{3,4},{4,5},{5,6},{6,7},{7,8},{8,9},{9,10},{10,1... | collective-permute-start | bytes 393224 | tf_op jit(solution)/shard_map/while/body/eval_jaxpr/ppermute | solution.py:13
  345.8 6.6 %collective-permute-start.2 = (f32[128,256]{0,1:T(8,128)S(1)}, f32[128,256]{0,1:T(8,128)S(1)}, u32[]{:S(2)}, u32[]{:S(2)}) collective-permute-start(f32[128,256]{0,1:T(8,128)S(1)} %maximum_add_fusion.4), channel_id=1, source_target_pairs={{0,1},{1,2},{2,3},{3,4},{4,5},{5,6},{6,7},{7,8},{8,9},{9,10},{10,1... | collective-permute-start | bytes 393224 | tf_op jit(solution)/shard_map/while/body/eval_jaxpr/ppermute | solution.py:13
  352.4 6.6 %collective-permute-start.3 = (f32[128,256]{0,1:T(8,128)S(1)}, f32[128,256]{0,1:T(8,128)S(1)}, u32[]{:S(2)}, u32[]{:S(2)}) collective-permute-start(f32[128,256]{0,1:T(8,128)S(1)} %maximum_add_fusion.5), channel_id=1, source_target_pairs={{0,1},{1,2},{2,3},{3,4},{4,5},{5,6},{6,7},{7,8},{8,9},{9,10},{10,1... | collective-permute-start | bytes 393224 | tf_op jit(solution)/shard_map/while/body/eval_jaxpr/ppermute | solution.py:13
  361.4 6.6 %collective-permute-start.2 = (f32[128,256]{0,1:T(8,128)S(1)}, f32[128,256]{0,1:T(8,128)S(1)}, u32[]{:S(2)}, u32[]{:S(2)}) collective-permute-start(f32[128,256]{0,1:T(8,128)S(1)} %maximum_add_fusion.4), channel_id=1, source_target_pairs={{0,1},{1,2},{2,3},{3,4},{4,5},{5,6},{6,7},{7,8},{8,9},{9,10},{10,1... | collective-permute-start | bytes 393224 | tf_op jit(solution)/shard_map/while/body/eval_jaxpr/ppermute | solution.py:13
  368.0 6.6 %collective-permute-start.3 = (f32[128,256]{0,1:T(8,128)S(1)}, f32[128,256]{0,1:T(8,128)S(1)}, u32[]{:S(2)}, u32[]{:S(2)}) collective-permute-start(f32[128,256]{0,1:T(8,128)S(1)} %maximum_add_fusion.5), channel_id=1, source_target_pairs={{0,1},{1,2},{2,3},{3,4},{4,5},{5,6},{6,7},{7,8},{8,9},{9,10},{10,1... | collective-permute-start | bytes 393224 | tf_op jit(solution)/shard_map/while/body/eval_jaxpr/ppermute | solution.py:13
  377.4 214.4 %all-reduce.2.cloned.1.call-start = ((), (), s32[]{:S(2)}) async-start(), calls=%async_computation.2 | async-start | bytes 262144 | tf_op jit(solution)/shard_map/psum | solution.py:136
  (111 other events, 902.6 us)
Sparse Core Ops, SparseCore 0:
  10.4 66.4 all-gather.2
  377.6 122.8 reduce-scatter.1
  503.1 88.6 all-reduce.1
where the time goes:
time: 601 us; the launch traced here: 600 us
  waiting for transfers between devices  433 us (72%)
  matrix products  82.5 us (14%)
  local copies, waits for them, and re-layouts  28.8 us (5%)
  other arithmetic  23.3 us (4%)
  between operations  13.9 us (2%)
  starting transfers between devices  10.3 us (2%)
  loops' own time  8.65 us (1%)
    ppermute x64, waiting for transfers between devices, from_behind(): lax.ppermute(x, axis, [(i, (i + by) % length) for i in range(length)])  155 us
    reduce_scatter x1, waiting for transfers between devices, on_device(): lax.psum_scatter(contract_rows(x_local, kv_grad_low), 'ctx', scatter_dime...  123 us
    psum x1, waiting for transfers between devices, on_device(): weight_total = lax.psum(weight_shard, 'dp')  90.5 us
    all_gather x1, waiting for transfers between devices, on_device(): kv_piece = lax.all_gather(kv_local, 'ctx', axis=0, tiled=True)  64.4 us
    dot_general x32, matrix products, backward_block(): jnp.dot(q_rows, kv_block[:, :HD].T, preferred_element_type=jnp.float32)  24.5 us
    dot_general x65, matrix products, contract_rows(): lax.dot_general(left_side, right_side, (((0,), (0,)), ((), ())), preferre...  20.6 us
    dot_general x32, matrix products, backward_block(): jnp.dot(low_score, kv_block[:, :HD], preferred_element_type=jnp.float32)  19.4 us
    reduce_sum x8, other arithmetic, forward_block(): new_sum = running_sum * factor + jnp.sum(expo_terms, axis=1)  13.4 us
  transfers between devices with their start and end apart: 67, of which 65 were waited for; matrix products, arithmetic and copies ran while one was open for 13% of the time, Pallas kernels for 0%

commit v1 on v0

--- a/solution.py
+++ b/solution.py
@@ -133,7 +133,7 @@
     weight_shard = lax.psum_scatter(
         contract_rows(x_local, kv_grad_low), "ctx", scatter_dimension=0, tiled=True
     )
-    weight_total = lax.psum(weight_shard, "dp")
+    weight_total = jnp.sum(lax.all_gather(weight_shard, "dp"), axis=0)
     return (grad_q_out, kv_grad_low.reshape(1, 1, local_count, 2 * HD), weight_total / dp_count)
 
 

time: 601 us -> 564 us (0.938)
  waiting for transfers between devices: 433 us -> 394 us
    psum x1 -> x0, waiting for transfers between devices: 90.5 us -> none  [on_device(): weight_total = lax.psum(weight_shard, 'dp')]
    all_gather x0 -> x1, waiting for transfers between devices: none -> 51.9 us  [on_device(): weight_total = jnp.sum(lax.all_gather(weight_shard, 'dp'), axis=0)]
  transfers between devices with their start and end apart: 67 -> 67, of which waited for: 65 -> 65; matrix products, arithmetic and copies ran while one was open for 13% -> 14% of each run, Pallas kernels for 0% -> 0%
where the time goes in v1:
time: 564 us; the launch traced here: 562 us
  waiting for transfers between devices  394 us (70%)
  matrix products  82.5 us (15%)
  local copies, waits for them, and re-layouts  30.2 us (5%)
  other arithmetic  22.7 us (4%)
  between operations  13.9 us (2%)
  starting transfers between devices  10.4 us (2%)
  loops' own time  8.67 us (2%)
    ppermute x64, waiting for transfers between devices, from_behind(): lax.ppermute(x, axis, [(i, (i + by) % length) for i in range(length)])  154 us
    reduce_scatter x1, waiting for transfers between devices, on_device(): lax.psum_scatter(contract_rows(x_local, kv_grad_low), 'ctx', scatter_dime...  123 us
    all_gather x1, waiting for transfers between devices, on_device(): kv_piece = lax.all_gather(kv_local, 'ctx', axis=0, tiled=True)  64.4 us
    all_gather x1, waiting for transfers between devices, on_device(): weight_total = jnp.sum(lax.all_gather(weight_shard, 'dp'), axis=0)  51.9 us
    dot_general x32, matrix products, backward_block(): jnp.dot(q_rows, kv_block[:, :HD].T, preferred_element_type=jnp.float32)  24.5 us
    dot_general x65, matrix products, contract_rows(): lax.dot_general(left_side, right_side, (((0,), (0,)), ((), ())), preferre...  20.5 us
    dot_general x32, matrix products, backward_block(): jnp.dot(low_score, kv_block[:, :HD], preferred_element_type=jnp.float32)  19.4 us
    reduce_sum x8, other arithmetic, forward_block(): new_sum = running_sum * factor + jnp.sum(expo_terms, axis=1)  13.4 us
  transfers between devices with their start and end apart: 67, of which 65 were waited for; matrix products, arithmetic and copies ran while one was open for 14% of the time, Pallas kernels for 0%

profile of v1, /device:TPU:32, one launch (start us, length us, event | category | flops | bytes accessed | tf_op | source)
XLA Modules:
  0.0 562.2 jit_solution(16175852171753326342)
XLA Ops:
  12.6 64.4 %all-gather.5.cloned.1.call-done = bf16[1,1,4096,256]{3,2,1,0:T(8,128)(2,1)} async-done(((bf16[1,1,128,256]{3,2,1,0:T(8,128)(2,1)}), bf16[1,1,4096,256]{3,2,1,0:T(8,128)(2,1)}) %all-gather.5.cloned.1.call-update) | async-done | bytes 2097168 | tf_op jit(solution)/shard_map/all_gather | solution.py:81
  77.0 55.6 %while.41 = (s32[]{:T(128)}, f32[1024]{0:T(1024)S(1)}, f32[1024]{0:T(1024)S(1)}, f32[1024]{0:T(1024)S(1)}, s32[8]{0:T(128)S(1)}, /*index=5*/s32[10]{0:T(128)S(1)...) while((s32[]{:T(128)}, f32[1024]{0:T(1024)S(1)}, ...), condition=%wide.region_7.8_spmd.clone, body=%wide.region_1.7_spmd.clone.sunk | while | flops 275166080 | bytes 18316680 | solution.py:89
  132.6 241.9 %while.42 = (s32[]{:T(128)}, f32[1024,128]{1,0:T(8,128)}, bf16[128,256]{1,0:T(8,128)(2,1)S(1)}, f32[128,256]{0,1:T(8,128)S(1)}, s32[]{:T(128)}, /*index=5*/s32[1...) while((s32[]{:T(128)}, f32[1024,128]{1,0:T(8,128)}, ...), condition=%wide.region_12.13_spmd.clone.clone.clone, body=%wide.region_8.12_spmd.clone.clone.clone.sunk | while | flops 338411936 | bytes 14973101 | solution.py:129
  166.2 3.0 collective-permute-done.1
  174.4 3.1 collective-permute-done
  181.8 3.0 collective-permute-done.1
  190.0 3.1 collective-permute-done
  197.4 3.0 collective-permute-done.1
  205.6 3.1 collective-permute-done
  213.0 3.0 collective-permute-done.1
  221.2 3.1 collective-permute-done
  228.6 3.0 collective-permute-done.1
  236.8 3.1 collective-permute-done
  244.2 3.0 collective-permute-done.1
  252.4 3.1 collective-permute-done
  259.8 3.0 collective-permute-done.1
  268.0 3.1 collective-permute-done
  275.4 3.0 collective-permute-done.1
  283.6 3.1 collective-permute-done
  291.0 3.0 collective-permute-done.1
  299.2 3.1 collective-permute-done
  306.6 3.0 collective-permute-done.1
  314.8 3.1 collective-permute-done
  322.2 3.0 collective-permute-done.1
  330.4 3.1 collective-permute-done
  337.8 3.0 collective-permute-done.1
  346.0 3.1 collective-permute-done
  353.4 3.0 collective-permute-done.1
  361.6 3.1 collective-permute-done
  369.0 3.0 collective-permute-done.1
  377.4 123.0 %reduce-scatter.2.cloned.1.call-done = f32[128,256]{0,1:T(8,128)} async-done(((f32[4096,256]{0,1:T(8,128)}), f32[128,256]{0,1:T(8,128)}) %reduce-scatter.2.cloned.1.call-update) | async-done | bytes 131088 | tf_op jit(solution)/shard_map/reduce_scatter | solution.py:133
  501.3 51.9 %all-gather.7.cloned.1.call-done = f32[1024,256]{0,1:T(8,128)} async-done(((f32[128,256]{0,1:T(8,128)}), f32[1024,256]{0,1:T(8,128)}) %all-gather.7.cloned.1.call-update) | async-done | bytes 1048592 | tf_op jit(solution)/shard_map/all_gather | solution.py:136
  (742 shorter events, 218.6 us)
Async XLA Ops:
  7.2 69.8 %all-gather.5.cloned.1.call-start = ((), (), s32[]{:S(2)}) async-start(), calls=%async_computation.2 | async-start | bytes 2162688 | tf_op jit(solution)/shard_map/all_gather | solution.py:81
  8.8 491.6 %reduce-scatter.2.cloned.1.call-start = ((), (), s32[]{:S(2)}) async-start(), calls=%async_computation.1 | async-start | bytes 4325376 | tf_op jit(solution)/shard_map/reduce_scatter | solution.py:133
  158.5 6.6 %collective-permute-start.2 = (f32[128,256]{0,1:T(8,128)S(1)}, f32[128,256]{0,1:T(8,128)S(1)}, u32[]{:S(2)}, u32[]{:S(2)}) collective-permute-start(f32[128,256]{0,1:T(8,128)S(1)} %maximum_add_fusion.4), channel_id=1, source_target_pairs={{0,1},{1,2},{2,3},{3,4},{4,5},{5,6},{6,7},{7,8},{8,9},{9,10},{10,1... | collective-permute-start | bytes 393224 | tf_op jit(solution)/shard_map/while/body/eval_jaxpr/ppermute | solution.py:13
  165.1 6.6 %collective-permute-start.3 = (f32[128,256]{0,1:T(8,128)S(1)}, f32[128,256]{0,1:T(8,128)S(1)}, u32[]{:S(2)}, u32[]{:S(2)}) collective-permute-start(f32[128,256]{0,1:T(8,128)S(1)} %maximum_add_fusion.5), channel_id=1, source_target_pairs={{0,1},{1,2},{2,3},{3,4},{4,5},{5,6},{6,7},{7,8},{8,9},{9,10},{10,1... | collective-permute-start | bytes 393224 | tf_op jit(solution)/shard_map/while/body/eval_jaxpr/ppermute | solution.py:13
  174.1 6.6 %collective-permute-start.2 = (f32[128,256]{0,1:T(8,128)S(1)}, f32[128,256]{0,1:T(8,128)S(1)}, u32[]{:S(2)}, u32[]{:S(2)}) collective-permute-start(f32[128,256]{0,1:T(8,128)S(1)} %maximum_add_fusion.4), channel_id=1, source_target_pairs={{0,1},{1,2},{2,3},{3,4},{4,5},{5,6},{6,7},{7,8},{8,9},{9,10},{10,1... | collective-permute-start | bytes 393224 | tf_op jit(solution)/shard_map/while/body/eval_jaxpr/ppermute | solution.py:13
  180.7 6.6 %collective-permute-start.3 = (f32[128,256]{0,1:T(8,128)S(1)}, f32[128,256]{0,1:T(8,128)S(1)}, u32[]{:S(2)}, u32[]{:S(2)}) collective-permute-start(f32[128,256]{0,1:T(8,128)S(1)} %maximum_add_fusion.5), channel_id=1, source_target_pairs={{0,1},{1,2},{2,3},{3,4},{4,5},{5,6},{6,7},{7,8},{8,9},{9,10},{10,1... | collective-permute-start | bytes 393224 | tf_op jit(solution)/shard_map/while/body/eval_jaxpr/ppermute | solution.py:13
  189.7 6.6 %collective-permute-start.2 = (f32[128,256]{0,1:T(8,128)S(1)}, f32[128,256]{0,1:T(8,128)S(1)}, u32[]{:S(2)}, u32[]{:S(2)}) collective-permute-start(f32[128,256]{0,1:T(8,128)S(1)} %maximum_add_fusion.4), channel_id=1, source_target_pairs={{0,1},{1,2},{2,3},{3,4},{4,5},{5,6},{6,7},{7,8},{8,9},{9,10},{10,1... | collective-permute-start | bytes 393224 | tf_op jit(solution)/shard_map/while/body/eval_jaxpr/ppermute | solution.py:13
  196.3 6.6 %collective-permute-start.3 = (f32[128,256]{0,1:T(8,128)S(1)}, f32[128,256]{0,1:T(8,128)S(1)}, u32[]{:S(2)}, u32[]{:S(2)}) collective-permute-start(f32[128,256]{0,1:T(8,128)S(1)} %maximum_add_fusion.5), channel_id=1, source_target_pairs={{0,1},{1,2},{2,3},{3,4},{4,5},{5,6},{6,7},{7,8},{8,9},{9,10},{10,1... | collective-permute-start | bytes 393224 | tf_op jit(solution)/shard_map/while/body/eval_jaxpr/ppermute | solution.py:13
  205.3 6.6 %collective-permute-start.2 = (f32[128,256]{0,1:T(8,128)S(1)}, f32[128,256]{0,1:T(8,128)S(1)}, u32[]{:S(2)}, u32[]{:S(2)}) collective-permute-start(f32[128,256]{0,1:T(8,128)S(1)} %maximum_add_fusion.4), channel_id=1, source_target_pairs={{0,1},{1,2},{2,3},{3,4},{4,5},{5,6},{6,7},{7,8},{8,9},{9,10},{10,1... | collective-permute-start | bytes 393224 | tf_op jit(solution)/shard_map/while/body/eval_jaxpr/ppermute | solution.py:13
  211.9 6.6 %collective-permute-start.3 = (f32[128,256]{0,1:T(8,128)S(1)}, f32[128,256]{0,1:T(8,128)S(1)}, u32[]{:S(2)}, u32[]{:S(2)}) collective-permute-start(f32[128,256]{0,1:T(8,128)S(1)} %maximum_add_fusion.5), channel_id=1, source_target_pairs={{0,1},{1,2},{2,3},{3,4},{4,5},{5,6},{6,7},{7,8},{8,9},{9,10},{10,1... | collective-permute-start | bytes 393224 | tf_op jit(solution)/shard_map/while/body/eval_jaxpr/ppermute | solution.py:13
  220.9 6.6 %collective-permute-start.2 = (f32[128,256]{0,1:T(8,128)S(1)}, f32[128,256]{0,1:T(8,128)S(1)}, u32[]{:S(2)}, u32[]{:S(2)}) collective-permute-start(f32[128,256]{0,1:T(8,128)S(1)} %maximum_add_fusion.4), channel_id=1, source_target_pairs={{0,1},{1,2},{2,3},{3,4},{4,5},{5,6},{6,7},{7,8},{8,9},{9,10},{10,1... | collective-permute-start | bytes 393224 | tf_op jit(solution)/shard_map/while/body/eval_jaxpr/ppermute | solution.py:13
  227.5 6.6 %collective-permute-start.3 = (f32[128,256]{0,1:T(8,128)S(1)}, f32[128,256]{0,1:T(8,128)S(1)}, u32[]{:S(2)}, u32[]{:S(2)}) collective-permute-start(f32[128,256]{0,1:T(8,128)S(1)} %maximum_add_fusion.5), channel_id=1, source_target_pairs={{0,1},{1,2},{2,3},{3,4},{4,5},{5,6},{6,7},{7,8},{8,9},{9,10},{10,1... | collective-permute-start | bytes 393224 | tf_op jit(solution)/shard_map/while/body/eval_jaxpr/ppermute | solution.py:13
  236.5 6.6 %collective-permute-start.2 = (f32[128,256]{0,1:T(8,128)S(1)}, f32[128,256]{0,1:T(8,128)S(1)}, u32[]{:S(2)}, u32[]{:S(2)}) collective-permute-start(f32[128,256]{0,1:T(8,128)S(1)} %maximum_add_fusion.4), channel_id=1, source_target_pairs={{0,1},{1,2},{2,3},{3,4},{4,5},{5,6},{6,7},{7,8},{8,9},{9,10},{10,1... | collective-permute-start | bytes 393224 | tf_op jit(solution)/shard_map/while/body/eval_jaxpr/ppermute | solution.py:13
  243.1 6.6 %collective-permute-start.3 = (f32[128,256]{0,1:T(8,128)S(1)}, f32[128,256]{0,1:T(8,128)S(1)}, u32[]{:S(2)}, u32[]{:S(2)}) collective-permute-start(f32[128,256]{0,1:T(8,128)S(1)} %maximum_add_fusion.5), channel_id=1, source_target_pairs={{0,1},{1,2},{2,3},{3,4},{4,5},{5,6},{6,7},{7,8},{8,9},{9,10},{10,1... | collective-permute-start | bytes 393224 | tf_op jit(solution)/shard_map/while/body/eval_jaxpr/ppermute | solution.py:13
  252.1 6.6 %collective-permute-start.2 = (f32[128,256]{0,1:T(8,128)S(1)}, f32[128,256]{0,1:T(8,128)S(1)}, u32[]{:S(2)}, u32[]{:S(2)}) collective-permute-start(f32[128,256]{0,1:T(8,128)S(1)} %maximum_add_fusion.4), channel_id=1, source_target_pairs={{0,1},{1,2},{2,3},{3,4},{4,5},{5,6},{6,7},{7,8},{8,9},{9,10},{10,1... | collective-permute-start | bytes 393224 | tf_op jit(solution)/shard_map/while/body/eval_jaxpr/ppermute | solution.py:13
  258.7 6.6 %collective-permute-start.3 = (f32[128,256]{0,1:T(8,128)S(1)}, f32[128,256]{0,1:T(8,128)S(1)}, u32[]{:S(2)}, u32[]{:S(2)}) collective-permute-start(f32[128,256]{0,1:T(8,128)S(1)} %maximum_add_fusion.5), channel_id=1, source_target_pairs={{0,1},{1,2},{2,3},{3,4},{4,5},{5,6},{6,7},{7,8},{8,9},{9,10},{10,1... | collective-permute-start | bytes 393224 | tf_op jit(solution)/shard_map/while/body/eval_jaxpr/ppermute | solution.py:13
  267.7 6.6 %collective-permute-start.2 = (f32[128,256]{0,1:T(8,128)S(1)}, f32[128,256]{0,1:T(8,128)S(1)}, u32[]{:S(2)}, u32[]{:S(2)}) collective-permute-start(f32[128,256]{0,1:T(8,128)S(1)} %maximum_add_fusion.4), channel_id=1, source_target_pairs={{0,1},{1,2},{2,3},{3,4},{4,5},{5,6},{6,7},{7,8},{8,9},{9,10},{10,1... | collective-permute-start | bytes 393224 | tf_op jit(solution)/shard_map/while/body/eval_jaxpr/ppermute | solution.py:13
  274.3 6.6 %collective-permute-start.3 = (f32[128,256]{0,1:T(8,128)S(1)}, f32[128,256]{0,1:T(8,128)S(1)}, u32[]{:S(2)}, u32[]{:S(2)}) collective-permute-start(f32[128,256]{0,1:T(8,128)S(1)} %maximum_add_fusion.5), channel_id=1, source_target_pairs={{0,1},{1,2},{2,3},{3,4},{4,5},{5,6},{6,7},{7,8},{8,9},{9,10},{10,1... | collective-permute-start | bytes 393224 | tf_op jit(solution)/shard_map/while/body/eval_jaxpr/ppermute | solution.py:13
  283.3 6.6 %collective-permute-start.2 = (f32[128,256]{0,1:T(8,128)S(1)}, f32[128,256]{0,1:T(8,128)S(1)}, u32[]{:S(2)}, u32[]{:S(2)}) collective-permute-start(f32[128,256]{0,1:T(8,128)S(1)} %maximum_add_fusion.4), channel_id=1, source_target_pairs={{0,1},{1,2},{2,3},{3,4},{4,5},{5,6},{6,7},{7,8},{8,9},{9,10},{10,1... | collective-permute-start | bytes 393224 | tf_op jit(solution)/shard_map/while/body/eval_jaxpr/ppermute | solution.py:13
  289.9 6.6 %collective-permute-start.3 = (f32[128,256]{0,1:T(8,128)S(1)}, f32[128,256]{0,1:T(8,128)S(1)}, u32[]{:S(2)}, u32[]{:S(2)}) collective-permute-start(f32[128,256]{0,1:T(8,128)S(1)} %maximum_add_fusion.5), channel_id=1, source_target_pairs={{0,1},{1,2},{2,3},{3,4},{4,5},{5,6},{6,7},{7,8},{8,9},{9,10},{10,1... | collective-permute-start | bytes 393224 | tf_op jit(solution)/shard_map/while/body/eval_jaxpr/ppermute | solution.py:13
  298.9 6.6 %collective-permute-start.2 = (f32[128,256]{0,1:T(8,128)S(1)}, f32[128,256]{0,1:T(8,128)S(1)}, u32[]{:S(2)}, u32[]{:S(2)}) collective-permute-start(f32[128,256]{0,1:T(8,128)S(1)} %maximum_add_fusion.4), channel_id=1, source_target_pairs={{0,1},{1,2},{2,3},{3,4},{4,5},{5,6},{6,7},{7,8},{8,9},{9,10},{10,1... | collective-permute-start | bytes 393224 | tf_op jit(solution)/shard_map/while/body/eval_jaxpr/ppermute | solution.py:13
  305.5 6.6 %collective-permute-start.3 = (f32[128,256]{0,1:T(8,128)S(1)}, f32[128,256]{0,1:T(8,128)S(1)}, u32[]{:S(2)}, u32[]{:S(2)}) collective-permute-start(f32[128,256]{0,1:T(8,128)S(1)} %maximum_add_fusion.5), channel_id=1, source_target_pairs={{0,1},{1,2},{2,3},{3,4},{4,5},{5,6},{6,7},{7,8},{8,9},{9,10},{10,1... | collective-permute-start | bytes 393224 | tf_op jit(solution)/shard_map/while/body/eval_jaxpr/ppermute | solution.py:13
  314.5 6.6 %collective-permute-start.2 = (f32[128,256]{0,1:T(8,128)S(1)}, f32[128,256]{0,1:T(8,128)S(1)}, u32[]{:S(2)}, u32[]{:S(2)}) collective-permute-start(f32[128,256]{0,1:T(8,128)S(1)} %maximum_add_fusion.4), channel_id=1, source_target_pairs={{0,1},{1,2},{2,3},{3,4},{4,5},{5,6},{6,7},{7,8},{8,9},{9,10},{10,1... | collective-permute-start | bytes 393224 | tf_op jit(solution)/shard_map/while/body/eval_jaxpr/ppermute | solution.py:13
  318.7 6.5 %collective-permute-start.1 = (bf16[128,256]{1,0:T(8,128)(2,1)S(1)}, bf16[128,256]{1,0:T(8,128)(2,1)S(1)}, u32[]{:S(2)}, u32[]{:S(2)}) collective-permute-start(bf16[128,256]{1,0:T(8,128)(2,1)S(1)} %collective-permute-done), channel_id=1, source_target_pairs={{0,1},{1,2},{2,3},{3,4},{4,5},{5,6},{6,7},{7,8},{8,9},{9,10},{10,1... | collective-permute-start | bytes 196616 | tf_op jit(solution)/shard_map/while/body/eval_jaxpr/ppermute | solution.py:13
  321.1 6.6 %collective-permute-start.3 = (f32[128,256]{0,1:T(8,128)S(1)}, f32[128,256]{0,1:T(8,128)S(1)}, u32[]{:S(2)}, u32[]{:S(2)}) collective-permute-start(f32[128,256]{0,1:T(8,128)S(1)} %maximum_add_fusion.5), channel_id=1, source_target_pairs={{0,1},{1,2},{2,3},{3,4},{4,5},{5,6},{6,7},{7,8},{8,9},{9,10},{10,1... | collective-permute-start | bytes 393224 | tf_op jit(solution)/shard_map/while/body/eval_jaxpr/ppermute | solution.py:13
  330.1 6.6 %collective-permute-start.2 = (f32[128,256]{0,1:T(8,128)S(1)}, f32[128,256]{0,1:T(8,128)S(1)}, u32[]{:S(2)}, u32[]{:S(2)}) collective-permute-start(f32[128,256]{0,1:T(8,128)S(1)} %maximum_add_fusion.4), channel_id=1, source_target_pairs={{0,1},{1,2},{2,3},{3,4},{4,5},{5,6},{6,7},{7,8},{8,9},{9,10},{10,1... | collective-permute-start | bytes 393224 | tf_op jit(solution)/shard_map/while/body/eval_jaxpr/ppermute | solution.py:13
  336.7 6.6 %collective-permute-start.3 = (f32[128,256]{0,1:T(8,128)S(1)}, f32[128,256]{0,1:T(8,128)S(1)}, u32[]{:S(2)}, u32[]{:S(2)}) collective-permute-start(f32[128,256]{0,1:T(8,128)S(1)} %maximum_add_fusion.5), channel_id=1, source_target_pairs={{0,1},{1,2},{2,3},{3,4},{4,5},{5,6},{6,7},{7,8},{8,9},{9,10},{10,1... | collective-permute-start | bytes 393224 | tf_op jit(solution)/shard_map/while/body/eval_jaxpr/ppermute | solution.py:13
  345.7 6.6 %collective-permute-start.2 = (f32[128,256]{0,1:T(8,128)S(1)}, f32[128,256]{0,1:T(8,128)S(1)}, u32[]{:S(2)}, u32[]{:S(2)}) collective-permute-start(f32[128,256]{0,1:T(8,128)S(1)} %maximum_add_fusion.4), channel_id=1, source_target_pairs={{0,1},{1,2},{2,3},{3,4},{4,5},{5,6},{6,7},{7,8},{8,9},{9,10},{10,1... | collective-permute-start | bytes 393224 | tf_op jit(solution)/shard_map/while/body/eval_jaxpr/ppermute | solution.py:13
  352.3 6.6 %collective-permute-start.3 = (f32[128,256]{0,1:T(8,128)S(1)}, f32[128,256]{0,1:T(8,128)S(1)}, u32[]{:S(2)}, u32[]{:S(2)}) collective-permute-start(f32[128,256]{0,1:T(8,128)S(1)} %maximum_add_fusion.5), channel_id=1, source_target_pairs={{0,1},{1,2},{2,3},{3,4},{4,5},{5,6},{6,7},{7,8},{8,9},{9,10},{10,1... | collective-permute-start | bytes 393224 | tf_op jit(solution)/shard_map/while/body/eval_jaxpr/ppermute | solution.py:13
  361.3 6.6 %collective-permute-start.2 = (f32[128,256]{0,1:T(8,128)S(1)}, f32[128,256]{0,1:T(8,128)S(1)}, u32[]{:S(2)}, u32[]{:S(2)}) collective-permute-start(f32[128,256]{0,1:T(8,128)S(1)} %maximum_add_fusion.4), channel_id=1, source_target_pairs={{0,1},{1,2},{2,3},{3,4},{4,5},{5,6},{6,7},{7,8},{8,9},{9,10},{10,1... | collective-permute-start | bytes 393224 | tf_op jit(solution)/shard_map/while/body/eval_jaxpr/ppermute | solution.py:13
  367.9 6.6 %collective-permute-start.3 = (f32[128,256]{0,1:T(8,128)S(1)}, f32[128,256]{0,1:T(8,128)S(1)}, u32[]{:S(2)}, u32[]{:S(2)}) collective-permute-start(f32[128,256]{0,1:T(8,128)S(1)} %maximum_add_fusion.5), channel_id=1, source_target_pairs={{0,1},{1,2},{2,3},{3,4},{4,5},{5,6},{6,7},{7,8},{8,9},{9,10},{10,1... | collective-permute-start | bytes 393224 | tf_op jit(solution)/shard_map/while/body/eval_jaxpr/ppermute | solution.py:13
  377.3 175.8 %all-gather.7.cloned.1.call-start = ((), (), s32[]{:S(2)}) async-start(), calls=%async_computation.3 | async-start | bytes 1179648 | tf_op jit(solution)/shard_map/all_gather | solution.py:136
  (111 other events, 902.3 us)
Sparse Core Ops, SparseCore 0:
  10.4 66.4 all-gather.4
  377.4 122.9 reduce-scatter.1
  502.9 50.2 all-gather.6
